TPU v7x, 512 devices: a whole 4x4x16 slice. The times are simulated.
512 devices in a mesh: segment: 4 (over x_hi, core), seq: 32 (over x_lo, z), dp: 4 (over y).
Axes of the slice: x: 4 (x_hi: 2, x_lo: 2; x = x_hi * 2 + x_lo), y: 4, z: 16, core: 2. Of those that a mesh axis runs over, the one named last changes fastest.
Arguments:
- q_in: bfloat16 [4, 4096, 1536], P('dp', 'seq', 'segment'), may hold values from -128 to 128
- k_in: bfloat16 [4, 4096, 1536], P('dp', 'seq', 'segment'), may hold values from -128 to 128
- v_in: bfloat16 [4, 4096, 1536], P('dp', 'seq', 'segment'), may hold values from -6 to 6
- q_gain: float32 [2, 64], replicated, may hold values from 1.5 to 4
- gate: float32 [768], replicated, may hold values from -6 to 6
- cot: bfloat16 [4, 4096, 768], P('dp', 'seq'), may hold values from -6 to 6
Outputs:
- attn_out: bfloat16 [4, 4096, 1536], P('dp', 'seq', 'segment')
- grad_gate: float32 [768], replicated
All inputs are finite; a program needn't handle non-finite values.
Results may differ from a plain program's by a relative error of at most 0.028.
The roundings to bfloat16 on the way count: a program that leaves them out, or rounds other values in their place, can miss the bound.
Values may be sent and summed in bfloat16 or wider, within the bound.
A program may use at most 64 MiB of HBM per device.

v0:
```python
import jax
import jax.numpy as jnp
from jax import lax
from jax.sharding import PartitionSpec as P

HEAD_DIM = 64


def shifted(value, axis, steps):
    count = lax.axis_size(axis)
    first, last = (max(0, -steps), min(count, count - steps))
    return lax.ppermute(value, axis, [(source, source + steps) for source in range(first, last)])


def attend(query, all_keys, all_values):
    count_rows = query.shape[0]
    total_keys = all_keys.shape[0]
    span = 2 * HEAD_DIM
    pieces = []
    probs_list = []
    totals_list = []
    for offset in range(0, query.shape[1], span):
        query_group = query[:, offset : offset + span].reshape(count_rows, 2, HEAD_DIM)
        keys_group = all_keys[:, offset : offset + span].reshape(total_keys, 2, HEAD_DIM)
        values_group = all_values[:, offset : offset + span].reshape(total_keys, 2, HEAD_DIM)
        scores = jnp.einsum(
            "qhd,khd->hqk", query_group, keys_group, preferred_element_type=jnp.float32
        ) * HEAD_DIM ** (-0.5)
        peak = jnp.max(scores, axis=-1, keepdims=True)
        expd = jnp.exp(scores - peak)
        total = jnp.sum(expd, axis=-1, keepdims=True)
        probs = expd.astype(jnp.bfloat16)
        result = jnp.einsum("hqk,khd->qhd", probs, values_group, preferred_element_type=jnp.float32)
        result = result / jnp.transpose(total, (1, 0, 2))
        pieces.append(result.reshape(count_rows, span))
        probs_list.append(probs)
        totals_list.append(total)
    return (jnp.concatenate(pieces, axis=1), probs_list, totals_list)


def attend_back(probs_list, totals_list, normed, upstream, all_keys, all_values):
    count_rows = upstream.shape[0]
    total_keys = all_keys.shape[0]
    span = 2 * HEAD_DIM
    pieces = []
    for number in range(len(probs_list)):
        offset = number * span
        upstream_group = upstream[:, offset : offset + span].reshape(count_rows, 2, HEAD_DIM)
        normed_group = normed[:, offset : offset + span].reshape(count_rows, 2, HEAD_DIM)
        keys_group = all_keys[:, offset : offset + span].reshape(total_keys, 2, HEAD_DIM)
        values_group = all_values[:, offset : offset + span].reshape(total_keys, 2, HEAD_DIM)
        dprob = jnp.einsum(
            "qhd,khd->hqk", upstream_group, values_group, preferred_element_type=jnp.float32
        )
        delta = jnp.sum(upstream_group.astype(jnp.float32) * normed_group, axis=-1)
        delta = jnp.transpose(delta, (1, 0))[:, :, None]
        dscore = (
            probs_list[number].astype(jnp.float32) / totals_list[number] * (dprob - delta)
        ).astype(jnp.bfloat16)
        result = jnp.einsum(
            "hqk,khd->qhd", dscore, keys_group, preferred_element_type=jnp.float32
        ) * HEAD_DIM ** (-0.5)
        pieces.append(result.reshape(count_rows, span))
    return jnp.concatenate(pieces, axis=1)


def local(q_in, k_in, v_in, q_gain, gate, cot):
    half = lax.axis_size("segment") // 2
    place = lax.axis_index("segment")
    is_main = place >= half
    section = place // half
    slot = place % half
    queries = q_in[0]
    keys = k_in[0]
    values = v_in[0]
    count_rows = queries.shape[0]
    width_dev = queries.shape[1]
    all_keys, all_values = (
        lax.all_gather(keys, "seq", axis=0, tiled=True),
        lax.all_gather(values, "seq", axis=0, tiled=True),
    )
    gain_row = lax.dynamic_slice_in_dim(q_gain, section, 1, 0)[0]
    gate_part = lax.dynamic_slice_in_dim(gate, slot * width_dev, width_dev, 0)
    cot_part = lax.dynamic_slice_in_dim(cot[0], slot * width_dev, width_dev, 1)
    raw = queries.astype(jnp.float32).reshape(count_rows, width_dev // HEAD_DIM, HEAD_DIM)
    unit = raw * lax.rsqrt(jnp.mean(raw * raw, axis=-1, keepdims=True) + 1e-06)
    base = (unit * gain_row).reshape(count_rows, width_dev)

    def control_run(base_in):
        normed_c = attend(base_in.astype(jnp.bfloat16), all_keys, all_values)[0]
        return lax.optimization_barrier(normed_c.astype(jnp.bfloat16))

    def control_skip(base_in):
        return jnp.zeros((count_rows, width_dev), jnp.bfloat16)

    first = lax.cond(is_main, control_skip, control_run, base)
    first_wide = first.astype(jnp.float32)
    outgoing = (gate_part * first_wide).astype(jnp.bfloat16)
    incoming = shifted(outgoing, "segment", half)

    def main_run(incoming_in):
        query = (base + incoming_in.astype(jnp.float32)).astype(jnp.bfloat16)
        normed_m, probs_list, totals_list = attend(query, all_keys, all_values)
        dquery = attend_back(probs_list, totals_list, normed_m, cot_part, all_keys, all_values)
        return (normed_m.astype(jnp.bfloat16), dquery)

    def main_skip(incoming_in):
        return (
            jnp.zeros((count_rows, width_dev), jnp.bfloat16),
            jnp.zeros((count_rows, width_dev), jnp.float32),
        )

    final, dquery_main = lax.cond(is_main, main_run, main_skip, incoming)
    returned = shifted(dquery_main.astype(jnp.bfloat16), "segment", -half)
    returned_wide = returned.astype(jnp.float32)
    part_gate = jnp.sum(first_wide * returned_wide, axis=0)
    placed = lax.dynamic_update_slice_in_dim(
        jnp.zeros((width_dev * half,), jnp.float32), part_gate, slot * width_dev, 0
    )
    total_gate = lax.psum(placed, ("segment", "seq", "dp"))
    output = jnp.where(is_main, final, first)
    return (output[None], total_gate)


def solution(mesh):
    in_specs = (
        P("dp", "seq", "segment"),
        P("dp", "seq", "segment"),
        P("dp", "seq", "segment"),
        P(),
        P(),
        P("dp", "seq", None),
    )
    out_specs = (P("dp", "seq", "segment"), P())
    return jax.shard_map(local, mesh=mesh, in_specs=in_specs, out_specs=out_specs, check_vma=False)
```

profile of v0, /device:TPU:1, one launch (start us, length us, event | category | flops | bytes accessed | tf_op | source)
XLA Modules:
  0.0 449.7 jit_solution(1224437534765963869)
XLA Ops:
  7.2 1.6 copy.10
  8.9 0.0 all-gather.7.cloned.1.call-start
  8.9 1.6 copy.11
  10.6 0.1 mul.127
  10.7 1.0 copy.9
  11.8 0.1 fusion.70
  11.9 0.8 dynamic_slice.11
  12.7 116.3 %all-gather.5.cloned.1.call-done = bf16[1,4096,384]{1,2,0:T(8,128)(2,1)} async-done(((bf16[1,128,384]{1,2,0:T(8,128)(2,1)}), bf16[1,4096,384]{1,2,0:T(8,128)(2,1)}) %all-gather.5.cloned.1.call-update) | async-done | bytes 3145744 | tf_op jit(solution)/shard_map/all_gather | solution.py:79
  129.0 133.1 %all-gather.7.cloned.1.call-done = bf16[1,4096,384]{1,2,0:T(8,128)(2,1)} async-done(((bf16[1,128,384]{1,2,0:T(8,128)(2,1)}), bf16[1,4096,384]{1,2,0:T(8,128)(2,1)}) %all-gather.7.cloned.1.call-update) | async-done | bytes 3145744 | tf_op jit(solution)/shard_map/all_gather | solution.py:80
  262.1 10.9 %conditional.2 = (f32[128,384]{0,1:T(8,128)S(1)}, bf16[128,384]{1,0:T(8,128)(2,1)S(1)}) conditional(s32[]{:T(128)} %convert_element_type.105, (f32[128,384]{0,1:T(8,128)S(1)}, bf16[4096,384]{0,1:T(8,128)(2,1)}, bf16[4096,384]{0,1:T(8,128)(2,1)}) %tuple.81, () %tuple.30), branch_computations={%region_1.8_spmd, %region_8.9_spmd} | conditional | flops 824670720 | bytes 58014736 | solution.py:96
  262.1 3.2 fusion.71
  265.4 0.8 fusion.76
  266.2 0.7 fusion
  267.0 0.9 fusion.39
  267.9 0.8 fusion.75
  268.7 0.7 fusion.2
  269.4 0.9 fusion.36
  270.4 0.8 fusion.74
  271.2 0.7 fusion.4
  271.9 0.9 fusion.33
  272.9 0.1 copy.15
  273.1 0.1 multiply_convert_fusion
  273.2 1.3 collective-permute-start
  274.5 1.6 collective-permute-done
  276.1 0.9 conditional.3
  276.1 0.7 broadcast.53.clone
  277.0 1.3 collective-permute-start.1
  278.3 1.6 select_bitcast_fusion
  279.8 38.2 %collective-permute-done.1 = bf16[128,384]{0,1:T(8,128)(2,1)S(1)} collective-permute-done((bf16[128,384]{0,1:T(8,128)(2,1)S(1)}, bf16[128,384]{0,1:T(8,128)(2,1)S(1)}, u32[]{:S(2)}, u32[]{:S(2)}) %collective-permute-start.1) | collective-permute-done | bytes 98336 | tf_op jit(solution)/shard_map/ppermute | solution.py:12
  318.0 0.1 multiply_reduce_fusion.3
  318.2 0.2 dynamic_update_slice.3
  318.5 124.4 %psum.7 = f32[768]{0:T(1024)} all-reduce(f32[768]{0:T(1024)S(1)} %dynamic_update_slice.3), channel_id=1, replica_groups=mesh['segment'=4,'seq'=32,'dp'=4] {'segment','seq','dp'}, use_global_device_ids=true, to_apply=%region_21.22 | all-reduce | flops 768 | bytes 6144 | tf_op jit(solution)/shard_map/psum | solution.py:120
  (18 shorter events, 0.2 us)
Async XLA Ops:
  7.2 3.4 copy-start
  7.2 121.8 %all-gather.5.cloned.1.call-start = ((), (), s32[]{:S(2)}) async-start(), calls=%async_computation | async-start | bytes 3244032 | tf_op jit(solution)/shard_map/all_gather | solution.py:79
  8.9 253.3 %all-gather.7.cloned.1.call-start = ((), (), s32[]{:S(2)}) async-start(), calls=%async_computation.1 | async-start | bytes 3244032 | tf_op jit(solution)/shard_map/all_gather | solution.py:80
  273.1 3.1 copy-start.6
  273.2 2.9 collective-permute-start
  277.0 41.1 %collective-permute-start.1 = (bf16[128,384]{0,1:T(8,128)(2,1)S(1)}, bf16[128,384]{0,1:T(8,128)(2,1)S(1)}, u32[]{:S(2)}, u32[]{:S(2)}) collective-permute-start(bf16[128,384]{0,1:T(8,128)(2,1)S(1)} %get-tuple-element.53), channel_id=1, source_target_pairs={{256,0},{384,128},{257,1},{385,129},{258,2},{386,130},{259,3},{387... | collective-permute-start | bytes 294920 | tf_op jit(solution)/shard_map/ppermute | solution.py:12
Sparse Core Ops, SparseCore 0:
  10.6 118.3 all-gather.4
  131.0 131.0 all-gather.6
where the time goes:
time: 450 us
  waiting for transfers between devices  289 us (64%)
  blocking collectives  124 us (28%)
  between operations  14.2 us (3%)
  local copies, waits for them, and re-layouts  9.4 us (2%)
  matrix products  5.29 us (1%)
    all_gather x1, waiting for transfers between devices, local(): lax.all_gather(values, 'seq', axis=0, tiled=True)  133 us
    psum x1, blocking collectives, local(): total_gate = lax.psum(placed, ('segment', 'seq', 'dp'))  124 us
    all_gather x1, waiting for transfers between devices, local(): lax.all_gather(keys, 'seq', axis=0, tiled=True)  116 us
    ppermute x2, waiting for transfers between devices, shifted(): lax.ppermute(value, axis, [(source, source + steps) for source in range(f...  39.8 us
  transfers between devices with their start and end apart: 4, of which 4 were waited for; matrix products, arithmetic and copies ran while one was open for 1% of the time, Pallas kernels for 0%

commit v1 on v0

v1 whole, which is shorter than its diff:
```python
import functools

import jax
import jax.numpy as jnp
from jax import lax
from jax.experimental import pallas as pl
from jax.experimental.pallas import tpu as pltpu
from jax.sharding import PartitionSpec as P

MESH = pl.DeviceIdType.MESH
HD = 64
NH = 3
TOK = 128
NZ = 16
KEYS = 4096
ROWS = 2 * TOK
CHUNK = 512
SCALE = HD ** (-0.5)
f32 = jnp.float32
bf16 = jnp.bfloat16


def kernel(
    q_ref, k_ref, v_ref, gain_ref, gate_ref, cot_ref,
    out_ref, gg_ref,
    pack_kv, pack_q, kv, qc, ac, fo, fp, scores, probs, ar1, ar2, ar3,
    ring_s, ring_r, xkv_s, xkv_r, xq_s, xq_r, ac_s, ac_r, fo_s, fo_r,
    ar1_s, ar1_r, ar2_s, ar2_r, ar3_s, ar3_r,
):
    seg = lax.axis_index("segment")
    seq = lax.axis_index("seq")
    dp = lax.axis_index("dp")
    xl = seq // NZ
    z = seq % NZ
    slot = seg % 2
    is_main = seg >= 2
    right = xl * NZ + (z + 1) % NZ
    left = xl * NZ + (z + NZ - 1) % NZ
    xpart = (1 - xl) * NZ + z
    across = (seg + 2) % 4

    barrier = pltpu.get_barrier_semaphore()
    for n in range(1, NZ):
        pl.semaphore_signal(
            barrier, inc=1, device_id={"seq": xl * NZ + (z + n) % NZ}, device_id_type=MESH
        )
    for n in range(1, 4):
        pl.semaphore_signal(barrier, inc=1, device_id={"dp": (dp + n) % 4}, device_id_type=MESH)
    for n in range(1, 8):
        pl.semaphore_signal(
            barrier,
            inc=1,
            device_id={"segment": (seg + n) % 4, "seq": ((xl + n // 4) % 2) * NZ + z},
            device_id_type=MESH,
        )

    for pair in range(3):
        cols = slice(pair * 128, pair * 128 + 128)
        kt, vt, qt = k_ref[0, :, cols], v_ref[0, :, cols], q_ref[0, :, cols]
        ct = cot_ref[0, :, pl.ds(pl.multiple_of(slot * 384 + pair * 128, 128), 128)]
        pack_kv[2 * pair] = jnp.concatenate([kt[:, :HD], vt[:, :HD]], axis=1)
        pack_kv[2 * pair + 1] = jnp.concatenate([kt[:, HD:], vt[:, HD:]], axis=1)
        pack_q[2 * pair] = jnp.concatenate([qt[:, :HD], ct[:, :HD]], axis=1)
        pack_q[2 * pair + 1] = jnp.concatenate([qt[:, HD:], ct[:, HD:]], axis=1)

    def place(zz, half):
        return pl.ds(pl.multiple_of((zz * 2 + half) * TOK, TOK), TOK)

    ar1[z] = jnp.zeros((8, 128), f32)
    for h in range(NH):
        kv[h, place(z, xl)] = pack_kv[xl * NH + h]
        qc[h, pl.ds(pl.multiple_of(xl * TOK, TOK), TOK)] = pack_q[xl * NH + h]

    pl.semaphore_wait(barrier, 25)

    def xkv_copy(h):
        return pltpu.make_async_remote_copy(
            src_ref=pack_kv.at[(1 - xl) * NH + h], dst_ref=kv.at[h, place(z, xl)],
            send_sem=xkv_s.at[h], recv_sem=xkv_r.at[h],
            device_id={"seq": xpart}, device_id_type=MESH,
        )

    def xq_copy(h):
        return pltpu.make_async_remote_copy(
            src_ref=pack_q.at[(1 - xl) * NH + h],
            dst_ref=qc.at[h, pl.ds(pl.multiple_of(xl * TOK, TOK), TOK)],
            send_sem=xq_s.at[h], recv_sem=xq_r.at[h],
            device_id={"seq": xpart}, device_id_type=MESH,
        )

    def ring_copy(h, zz, o, way):
        where = place(zz, (xl + o) % 2)
        return pltpu.make_async_remote_copy(
            src_ref=kv.at[h, where], dst_ref=kv.at[h, where],
            send_sem=ring_s.at[way, h, zz * 2 + o], recv_sem=ring_r.at[way, h, zz * 2 + o],
            device_id={"seq": right if way == 0 else left}, device_id_type=MESH,
        )

    for h in range(NH):
        xkv_copy(h).start()
    for h in range(NH):
        xq_copy(h).start()

    def at(j, way):
        return (z - j + NZ) % NZ if way == 0 else (z + j) % NZ

    for o in range(2):
        for h in range(NH):
            if o == 1:
                xkv_copy(h).wait_recv()
            for way in range(2):
                ring_copy(h, z, o, way).start()

    def ring_step(j, carry):
        for o in range(2):
            for h in range(NH):
                for way in range(2):
                    ring_copy(h, at(j, way), o, way).wait_recv()

                    @pl.when((j < NZ // 2 - 1) | (way == o))
                    def _():
                        ring_copy(h, at(j, way), o, way).start()
        return carry

    lax.fori_loop(1, NZ // 2, ring_step, 0)
    for h in range(NH):
        for o in range(2):
            ring_copy(h, at(NZ // 2, o), o, o).wait_recv()
    for h in range(NH):
        xq_copy(h).wait_recv()

    zero_half = jnp.zeros((ROWS, HD), bf16)

    def base_of(h, row):
        raw = qc[h][:, :HD].astype(f32)
        unit = raw * lax.rsqrt(jnp.mean(raw * raw, axis=-1, keepdims=True) + 1e-06)
        return unit * gain_ref[row:row + 1, :]

    def forward(h, query, keep):
        wide = jnp.concatenate([query * jnp.asarray(SCALE, bf16), zero_half], axis=1)

        def score_step(c, top):
            cols = pl.ds(pl.multiple_of(c * CHUNK, CHUNK), CHUNK)
            s = lax.dot_general(
                wide, kv[h, cols], (((1,), (1,)), ((), ())), preferred_element_type=f32
            )
            scores[:, cols] = s
            for i in range(CHUNK // 128):
                top = jnp.maximum(top, s[:, i * 128:(i + 1) * 128])
            return top

        top = lax.fori_loop(
            0, KEYS // CHUNK, score_step, jnp.full((ROWS, 128), -jnp.inf, f32)
        )
        peak = jnp.max(top, axis=-1, keepdims=True)

        def value_step(c, carry):
            total, acc = carry
            cols = pl.ds(pl.multiple_of(c * CHUNK, CHUNK), CHUNK)
            e = jnp.exp(scores[:, cols] - peak)
            for i in range(CHUNK // 128):
                total = total + e[:, i * 128:(i + 1) * 128]
            p = e.astype(bf16)
            if keep:
                probs[:, cols] = p
            acc = acc + jnp.dot(p, kv[h, cols], preferred_element_type=f32)
            return total, acc

        total, acc = lax.fori_loop(
            0, KEYS // CHUNK, value_step,
            (jnp.zeros((ROWS, 128), f32), jnp.zeros((ROWS, 128), f32)),
        )
        total = jnp.sum(total, axis=-1, keepdims=True)
        return acc[:, HD:] / total, total

    def ac_copy(h):
        return pltpu.make_async_remote_copy(
            src_ref=fo.at[h], dst_ref=ac.at[h], send_sem=ac_s.at[h], recv_sem=ac_r.at[h],
            device_id={"segment": across}, device_id_type=MESH,
        )

    def fo_copy(h):
        return pltpu.make_async_remote_copy(
            src_ref=fo.at[h], dst_ref=fp.at[h], send_sem=fo_s.at[h], recv_sem=fo_r.at[h],
            device_id={"seq": xpart}, device_id_type=MESH,
        )

    def folded(x):
        return jnp.concatenate([x[:TOK], x[TOK:]], axis=1)

    @pl.when(jnp.logical_not(is_main))
    def _():
        for h in range(NH):
            normed, _ = forward(h, base_of(h, 0).astype(bf16), False)
            fo[h] = folded(normed.astype(bf16))
            ac_copy(h).start()
            fo_copy(h).start()
        for h in range(NH):
            ac_copy(h).wait_send()

    def ar1_copy(n, src):
        return pltpu.make_async_remote_copy(
            src_ref=ar1.at[src], dst_ref=ar1.at[src],
            send_sem=ar1_s.at[n], recv_sem=ar1_r.at[src],
            device_id={"seq": xl * NZ + (z + n) % NZ}, device_id_type=MESH,
        )

    def ar2_copy(n, src):
        return pltpu.make_async_remote_copy(
            src_ref=ar2.at[src], dst_ref=ar2.at[src],
            send_sem=ar2_s.at[n], recv_sem=ar2_r.at[src],
            device_id={"dp": (dp + n) % 4}, device_id_type=MESH,
        )

    def ar3_copy(n, src):
        return pltpu.make_async_remote_copy(
            src_ref=ar3.at[src], dst_ref=ar3.at[src],
            send_sem=ar3_s.at[n], recv_sem=ar3_r.at[src],
            device_id={"segment": (seg + n) % 4, "seq": ((xl + n // 4) % 2) * NZ + z},
            device_id_type=MESH,
        )

    @pl.when(is_main)
    def _():
        for h in range(NH):
            base = base_of(h, 1)
            first = slot * 384 + xl * (NH * HD) + h * HD
            tile = gate_ref[:, pl.ds(pl.multiple_of((first // 128) * 128, 128), 128)]
            gate = jnp.where((xl + h) % 2 == 1, tile[:, HD:], tile[:, :HD])
            ac_copy(h).wait_recv()
            pair = ac[h]
            first_wide = jnp.concatenate([pair[:, :HD], pair[:, HD:]], axis=0).astype(f32)
            residual = (gate * first_wide).astype(bf16)
            query = (base + residual.astype(f32)).astype(bf16)
            normed, total = forward(h, query, True)
            fo[h] = folded(normed.astype(bf16))
            fo_copy(h).start()
            upstream = qc[h][:, HD:]
            wide = jnp.concatenate([zero_half, upstream], axis=1)
            delta = jnp.sum(upstream.astype(f32) * normed, axis=-1, keepdims=True)
            inverse = 1.0 / total

            def back_step(c, acc):
                cols = pl.ds(pl.multiple_of(c * CHUNK, CHUNK), CHUNK)
                block = kv[h, cols]
                dprob = lax.dot_general(
                    wide, block, (((1,), (1,)), ((), ())), preferred_element_type=f32
                )
                ds = (probs[:, cols].astype(f32) * inverse * (dprob - delta)).astype(bf16)
                return acc + jnp.dot(ds, block, preferred_element_type=f32)

            acc = lax.fori_loop(0, KEYS // CHUNK, back_step, jnp.zeros((ROWS, 128), f32))
            rgrad = (acc[:, :HD] * SCALE).astype(bf16).astype(f32)
            part = jnp.sum(first_wide * rgrad, axis=0, keepdims=True)
            ar1[z, h:h + 1, :] = jnp.concatenate([part, part], axis=1)

        for n in range(1, NZ):
            ar1_copy(n, z).start()
        for n in range(1, NZ):
            ar1_copy(n, (z + n) % NZ).wait_recv()
        part = ar1[0]
        for n in range(1, NZ):
            part = part + ar1[n]
        ar2[dp] = part
        for n in range(1, 4):
            ar2_copy(n, dp).start()
        for n in range(1, 4):
            ar2_copy(n, (dp + n) % 4).wait_recv()
        ar3[slot * 2 + xl] = (ar2[0] + ar2[1]) + (ar2[2] + ar2[3])
        for n in range(1, 8):
            ar3_copy(n, slot * 2 + xl).start()
        for n in range(1, 4):
            ar3_copy(n, (slot * 2 + xl + n) % 4).wait_recv()
        for n in range(1, NZ):
            ar1_copy(n, z).wait_send()
        for n in range(1, 4):
            ar2_copy(n, dp).wait_send()
        for n in range(1, 8):
            ar3_copy(n, slot * 2 + xl).wait_send()

    @pl.when(jnp.logical_not(is_main))
    def _():
        for n in range(4):
            ar3_copy(1, n).wait_recv()

    for group in range(4):
        for h in range(NH):
            first = group * NH * HD + h * HD
            low = (first % 128) // HD
            gg_ref[:, first:first + HD] = ar3[group, h:h + 1, low * HD:low * HD + HD]

    for h in range(NH):
        fo_copy(h).wait_recv()

    def assemble(lower, upper, half):
        cut = slice(half * HD, half * HD + HD)
        heads = [lower[h][:, cut] for h in range(NH)] + [upper[h][:, cut] for h in range(NH)]
        for pair in range(3):
            out_ref[0, :, pair * 128:pair * 128 + 128] = jnp.concatenate(
                [heads[2 * pair], heads[2 * pair + 1]], axis=1
            )

    @pl.when(xl == 0)
    def _():
        assemble(fo, fp, 0)

    @pl.when(xl == 1)
    def _():
        assemble(fp, fo, 1)

    for h in range(NH):
        fo_copy(h).wait_send()
        xkv_copy(h).wait_send()
        xq_copy(h).wait_send()

    def drain(j, carry):
        for h in range(NH):
            for o in range(2):
                for way in range(2):
                    @pl.when((j < NZ // 2 - 1) | (way == o))
                    def _():
                        ring_copy(h, at(j, way), o, way).wait_send()
        return carry

    lax.fori_loop(0, NZ // 2, drain, 0)


def local(q_in, k_in, v_in, q_gain, gate, cot):
    vmem = pl.BlockSpec(memory_space=pltpu.VMEM)
    dma = pltpu.SemaphoreType.DMA
    out, gg = pl.pallas_call(
        kernel,
        out_shape=(
            jax.ShapeDtypeStruct(q_in.shape, bf16),
            jax.ShapeDtypeStruct((1, gate.shape[0]), f32),
        ),
        in_specs=[vmem] * 6,
        out_specs=(vmem, vmem),
        scratch_shapes=[
            pltpu.VMEM((2 * NH, TOK, 128), bf16),
            pltpu.VMEM((2 * NH, TOK, 128), bf16),
            pltpu.VMEM((NH, KEYS, 128), bf16),
            pltpu.VMEM((NH, ROWS, 128), bf16),
            pltpu.VMEM((NH, TOK, 128), bf16),
            pltpu.VMEM((NH, TOK, 128), bf16),
            pltpu.VMEM((NH, TOK, 128), bf16),
            pltpu.VMEM((ROWS, KEYS), f32),
            pltpu.VMEM((ROWS, KEYS), bf16),
            pltpu.VMEM((NZ, 8, 128), f32),
            pltpu.VMEM((4, 8, 128), f32),
            pltpu.VMEM((4, 8, 128), f32),
            dma((2, NH, 2 * NZ)), dma((2, NH, 2 * NZ)),
            dma((NH,)), dma((NH,)), dma((NH,)), dma((NH,)),
            dma((NH,)), dma((NH,)), dma((NH,)), dma((NH,)),
            dma((NZ,)), dma((NZ,)), dma((4,)), dma((4,)), dma((8,)), dma((4,)),
        ],
        compiler_params=pltpu.CompilerParams(
            collective_id=0, has_side_effects=True, vmem_limit_bytes=48 * 2**20
        ),
    )(q_in, k_in, v_in, q_gain, gate.reshape(1, -1), cot)
    return out, gg.reshape(-1)


def solution(mesh):
    in_specs = (
        P("dp", "seq", "segment"),
        P("dp", "seq", "segment"),
        P("dp", "seq", "segment"),
        P(),
        P(),
        P("dp", "seq", None),
    )
    out_specs = (P("dp", "seq", "segment"), P())
    return jax.shard_map(local, mesh=mesh, in_specs=in_specs, out_specs=out_specs, check_vma=False)
```

time: 450 us -> 109 us (0.24)
  waiting for transfers between devices: 289 us -> 0 us
  blocking collectives: 124 us -> 0 us
  Pallas kernels: 0 us -> 103 us
  between operations: 14.2 us -> 0.65 us
  matrix products: 5.29 us -> 0 us
    all_gather x2 -> x0, waiting for transfers between devices: 249 us -> none  [the longest x1 133 us: local(): lax.all_gather(values, 'seq', axis=0, tiled=True)]
    psum x1 -> x0, blocking collectives: 124 us -> none  [local(): total_gate = lax.psum(placed, ('segment', 'seq', 'dp'))]
    pallas_call x0 -> x1, Pallas kernels: none -> 103 us  [local(): pl.pallas_call(kernel, out_shape=(jax.ShapeDtypeStruct(q_in.shape, bf16),...]
    ppermute x2 -> x0, waiting for transfers between devices: 39.8 us -> none  [shifted(): lax.ppermute(value, axis, [(source, source + steps) for source in range(f...]
    dot_general x6 -> x0, matrix products: 5.29 us -> none  [the longest x3 2.79 us: attend(): jnp.einsum('hqk,khd->qhd', probs, values_group, preferred_element_type=jn...]
  transfers between devices with their start and end apart: 4 -> 0, of which waited for: 4 -> 0; matrix products, arithmetic and copies ran while one was open for 1% -> 0% of each run, Pallas kernels for 0% -> 0%
where the time goes in v1:
time: 109 us
  Pallas kernels  103 us (94%)
  local copies, waits for them, and re-layouts  4.94 us (5%)
    pallas_call x1, Pallas kernels, local(): pl.pallas_call(kernel, out_shape=(jax.ShapeDtypeStruct(q_in.shape, bf16),...  103 us
    unnamed x11, local copies, waits for them, and re-layouts  4.25 us

profile of v1, /device:TPU:1, one launch (start us, length us, event | category | flops | bytes accessed | tf_op | source)
XLA Modules:
  0.0 108.8 jit_solution(7935496872597212325)
XLA Ops:
  0.6 0.0 copy-start.4
  0.6 0.7 reshape.10.gate_ref
  1.3 0.0 copy-done.4
  1.3 0.0 copy-start
  1.3 0.9 copy-done
  2.3 0.0 copy-start.1
  2.3 0.9 copy-done.1
  3.2 0.0 copy-start.2
  3.2 0.9 copy-done.2
  4.1 0.0 copy-start.3
  4.1 0.9 copy-done.3
  4.9 102.6 %shard_map.77 = (bf16[1,128,384]{2,1,0:T(8,128)(2,1)S(1)}, f32[1,768]{1,0:T(1,128)S(1)}) custom-call(bf16[1,128,384]{2,1,0:T(8,128)(2,1)S(1)} %copy-done.1, bf16[1,128,384]{2,1,0:T(8,128)(2,1)S(1)} %copy-done.2, bf16[1,128,384]{2,1,0:T(8,128)(2,1)S(1)} %copy-done.3, f32[2,64]{1,0:T(2,128)S(1)} %copy-done.4, f32[1,768]{1,0:T(1,128)S(1)} %reshape.10.gate_ref, ...), custom_call_target="tpu_custom_call" | custom-call | tf_op jit(solution)/shard_map/pallas_call | solution.py:331
  107.5 0.6 reduce
  108.1 0.6 copy.9
Async XLA Ops:
  0.6 0.7 copy-start.4
  1.3 0.9 copy-start
  2.3 0.9 copy-start.1
  3.2 0.9 copy-start.2
  4.1 0.9 copy-start.3

commit v2 on v1

--- a/solution.py
+++ b/solution.py
@@ -14,15 +14,16 @@
 NZ = 16
 KEYS = 4096
 ROWS = 2 * TOK
-CHUNK = 512
+CHUNK = 4096
 SCALE = HD ** (-0.5)
 f32 = jnp.float32
 bf16 = jnp.bfloat16
 
 
 def kernel(
-    q_ref, k_ref, v_ref, gain_ref, gate_ref, cot_ref,
+    q_hbm, k_hbm, v_hbm, gain_ref, gate_ref, cot_hbm,
     out_ref, gg_ref,
+    q_ref, k_ref, v_ref, cot_ref, load_s,
     pack_kv, pack_q, kv, qc, ac, fo, fp, scores, probs, ar1, ar2, ar3,
     ring_s, ring_r, xkv_s, xkv_r, xq_s, xq_r, ac_s, ac_r, fo_s, fo_r,
     ar1_s, ar1_r, ar2_s, ar2_r, ar3_s, ar3_r,
@@ -39,6 +40,15 @@
     xpart = (1 - xl) * NZ + z
     across = (seg + 2) % 4
 
+    loads = [
+        pltpu.make_async_copy(src, dst, load_s.at[n])
+        for n, (src, dst) in enumerate(
+            ((k_hbm, k_ref), (v_hbm, v_ref), (q_hbm, q_ref), (cot_hbm, cot_ref))
+        )
+    ]
+    for load in loads:
+        load.start()
+
     barrier = pltpu.get_barrier_semaphore()
     for n in range(1, NZ):
         pl.semaphore_signal(
@@ -54,6 +64,8 @@
             device_id_type=MESH,
         )
 
+    for load in loads:
+        load.wait()
     for pair in range(3):
         cols = slice(pair * 128, pair * 128 + 128)
         kt, vt, qt = k_ref[0, :, cols], v_ref[0, :, cols], q_ref[0, :, cols]
@@ -190,11 +202,14 @@
 
     @pl.when(jnp.logical_not(is_main))
     def _():
-        for h in range(NH):
+        def control_head(h, carry):
             normed, _ = forward(h, base_of(h, 0).astype(bf16), False)
             fo[h] = folded(normed.astype(bf16))
             ac_copy(h).start()
             fo_copy(h).start()
+            return carry
+
+        lax.fori_loop(0, NH, control_head, 0)
         for h in range(NH):
             ac_copy(h).wait_send()
 
@@ -222,7 +237,7 @@
 
     @pl.when(is_main)
     def _():
-        for h in range(NH):
+        def main_head(h, carry):
             base = base_of(h, 1)
             first = slot * 384 + xl * (NH * HD) + h * HD
             tile = gate_ref[:, pl.ds(pl.multiple_of((first // 128) * 128, 128), 128)]
@@ -252,7 +267,10 @@
             acc = lax.fori_loop(0, KEYS // CHUNK, back_step, jnp.zeros((ROWS, 128), f32))
             rgrad = (acc[:, :HD] * SCALE).astype(bf16).astype(f32)
             part = jnp.sum(first_wide * rgrad, axis=0, keepdims=True)
-            ar1[z, h:h + 1, :] = jnp.concatenate([part, part], axis=1)
+            ar1[z, pl.ds(h, 1), :] = jnp.concatenate([part, part], axis=1)
+            return carry
+
+        lax.fori_loop(0, NH, main_head, 0)
 
         for n in range(1, NZ):
             ar1_copy(n, z).start()
@@ -326,6 +344,7 @@
 
 
 def local(q_in, k_in, v_in, q_gain, gate, cot):
+    hbm = pl.BlockSpec(memory_space=pltpu.HBM)
     vmem = pl.BlockSpec(memory_space=pltpu.VMEM)
     dma = pltpu.SemaphoreType.DMA
     out, gg = pl.pallas_call(
@@ -334,9 +353,14 @@
             jax.ShapeDtypeStruct(q_in.shape, bf16),
             jax.ShapeDtypeStruct((1, gate.shape[0]), f32),
         ),
-        in_specs=[vmem] * 6,
+        in_specs=[hbm] * 3 + [vmem] * 2 + [hbm],
         out_specs=(vmem, vmem),
         scratch_shapes=[
+            pltpu.VMEM(q_in.shape, bf16),
+            pltpu.VMEM(k_in.shape, bf16),
+            pltpu.VMEM(v_in.shape, bf16),
+            pltpu.VMEM(cot.shape, bf16),
+            pltpu.SemaphoreType.DMA((4,)),
             pltpu.VMEM((2 * NH, TOK, 128), bf16),
             pltpu.VMEM((2 * NH, TOK, 128), bf16),
             pltpu.VMEM((NH, KEYS, 128), bf16),

time: 109 us -> 95.1 us (0.87)
  Pallas kernels: 103 us -> 88.7 us
    pallas_call x1, Pallas kernels: 103 us -> 88.7 us  [local(): pl.pallas_call(kernel, out_shape=(jax.ShapeDtypeStruct(q_in.shape, bf16),...]
where the time goes in v2:
time: 95.1 us; the launch traced here: 94.9 us
  Pallas kernels  88.7 us (93%)
  local copies, waits for them, and re-layouts  4.94 us (5%)
    pallas_call x1, Pallas kernels, local(): pl.pallas_call(kernel, out_shape=(jax.ShapeDtypeStruct(q_in.shape, bf16),...  88.7 us
    unnamed x11, local copies, waits for them, and re-layouts  4.25 us

profile of v2, /device:TPU:1, one launch (start us, length us, event | category | flops | bytes accessed | tf_op | source)
XLA Modules:
  0.0 94.9 jit_solution(11325070902972604111)
XLA Ops:
  0.6 0.0 copy-start.4
  0.6 0.7 reshape.10.gate_ref
  1.3 0.0 copy-done.4
  1.3 0.0 copy-start
  1.3 0.9 copy-done
  2.3 0.0 copy-start.1
  2.3 0.9 copy-done.1
  3.2 0.0 copy-start.2
  3.2 0.9 copy-done.2
  4.1 0.0 copy-start.3
  4.1 0.9 copy-done.3
  4.9 88.7 %shard_map.77 = (bf16[1,128,384]{2,1,0:T(8,128)(2,1)S(1)}, f32[1,768]{1,0:T(1,128)S(1)}) custom-call(bf16[1,128,384]{2,1,0:T(8,128)(2,1)S(1)} %copy-done.1, bf16[1,128,384]{2,1,0:T(8,128)(2,1)S(1)} %copy-done.2, bf16[1,128,384]{2,1,0:T(8,128)(2,1)S(1)} %copy-done.3, f32[2,64]{1,0:T(2,128)S(1)} %copy-done.4, f32[1,768]{1,0:T(1,128)S(1)} %reshape.10.gate_ref, ...), custom_call_target="tpu_custom_call" | custom-call | tf_op jit(solution)/shard_map/pallas_call | solution.py:350
  93.6 0.6 reduce
  94.2 0.6 copy.9
Async XLA Ops:
  0.6 0.7 copy-start.4
  1.3 0.9 copy-start
  2.3 0.9 copy-start.1
  3.2 0.9 copy-start.2
  4.1 0.9 copy-start.3

commit v3 on v0

v3 whole, which is shorter than its diff:
```python
import functools

import jax
import jax.numpy as jnp
from jax import lax
from jax.experimental import pallas as pl
from jax.experimental.pallas import tpu as pltpu
from jax.sharding import PartitionSpec as P

MESH = pl.DeviceIdType.MESH
HD = 64
NH = 3
TOK = 128
NZ = 16
NQ = 4
NP = 16
KEYS = 4096
ROWS = 2 * TOK
CHUNK = 4096
SCALE = HD ** (-0.5)
f32 = jnp.float32
bf16 = jnp.bfloat16


def kernel(
    q_hbm, k_hbm, v_hbm, gain_ref, gate_ref, cot_hbm,
    out_ref, gg_ref,
    q_ref, k_ref, v_ref, cot_ref,
    pack_kv, pack_q, pack_c, kv, qb, cb, ac, fo, rp, scores, probs, dprob, parts, ar1, ar2,
    load_s, p1_s, p1_r, q_s, q_r, c_s, c_r, ag_s, ag_r, ac_s, ac_r, rp_s, rp_r,
    ar1_s, ar1_r, ar2_s, ar2_r,
):
    seg = lax.axis_index("segment")
    seq = lax.axis_index("seq")
    y = lax.axis_index("dp")
    xh, c = seg // 2, seg % 2
    x, z = seq // NZ, seq % NZ
    is_main = xh == 1
    zq, zs = z // 4, z % 4
    me = (y * 2 + x) * 2 + c
    itself = z == 12 * c + y

    loads = [
        pltpu.make_async_copy(src, dst, load_s.at[n])
        for n, (src, dst) in enumerate(
            ((k_hbm, k_ref), (v_hbm, v_ref), (q_hbm, q_ref), (cot_hbm, cot_ref))
        )
    ]
    for load in loads:
        load.start()

    def target(f):
        return {"segment": xh * 2 + zq % 2, "seq": x * NZ + 4 * (2 * c + f) + y, "dp": zs}

    def source(b):
        return {"segment": xh * 2 + zq // 2, "seq": x * NZ + y + 4 * c + 8 * b, "dp": zs}

    def in_row(p):
        return {"segment": xh * 2 + p % 2, "seq": ((p // 2) % 2) * NZ + z, "dp": p // 4}

    def in_column(n):
        there = (xh * NZ + z + n) % (2 * NZ)
        return {"segment": (there // NZ) * 2 + c, "seq": x * NZ + there % NZ}

    def stays(n):
        return itself & (c == n)

    barrier = pltpu.get_barrier_semaphore()

    def hello(device):
        pl.semaphore_signal(barrier, inc=1, device_id=device, device_id_type=MESH)

    for n in range(2):
        @pl.when(jnp.logical_not(stays(n)))
        def _():
            hello(target(n))
            hello(source(n))
    for n in range(1, NP):
        hello(in_row((me + n) % NP))
    for n in range(1, 2 * NZ):
        hello(in_column(n))

    def fold(a):
        return jnp.concatenate([a[:HD], a[HD:]], axis=1)

    def unfold(a):
        return jnp.concatenate([a[:, :HD], a[:, HD:]], axis=0)

    for load in loads:
        load.wait()
    for pair in range(3):
        cols = slice(pair * 128, pair * 128 + 128)
        kt, vt, qt = k_ref[0, :, cols], v_ref[0, :, cols], q_ref[0, :, cols]
        ct = cot_ref[0, :, pl.ds(pl.multiple_of(c * 384 + pair * 128, 128), 128)]
        for half in range(2):
            f, h = (2 * pair + half) // NH, (2 * pair + half) % NH
            lanes = slice(half * HD, half * HD + HD)
            pack_kv[f, h] = jnp.concatenate([kt[:, lanes], vt[:, lanes]], axis=1)
            pack_q[f, h] = fold(qt[:, lanes])
            pack_c[f, h] = fold(ct[:, lanes])

    def rows(p, b):
        return pl.ds(pl.multiple_of((p * 2 + b) * TOK, TOK), TOK)

    def whole(p):
        return pl.ds(pl.multiple_of(p * ROWS, ROWS), ROWS)

    def remote(src, dst, send, recv, device):
        return pltpu.make_async_remote_copy(
            src_ref=src, dst_ref=dst, send_sem=send, recv_sem=recv,
            device_id=device, device_id_type=MESH,
        )

    there = (zs * 2 + x) * 2 + zq % 2
    block = zq // 2

    def p1_send(h, f):
        return remote(
            pack_kv.at[f, h], kv.at[h, rows(there, block)], p1_s.at[f, h], p1_r.at[block, h],
            target(f),
        )

    def p1_wait(h, b):
        return remote(
            pack_kv.at[0, h], kv.at[h, rows(me, b)], p1_s.at[0, h], p1_r.at[b, h], source(b)
        )

    def q_send(f):
        return remote(pack_q.at[f], qb.at[block], q_s.at[f], q_r.at[block], target(f))

    def q_wait(b):
        return remote(pack_q.at[0], qb.at[b], q_s.at[0], q_r.at[b], source(b))

    def c_send(f):
        return remote(pack_c.at[f], cb.at[block], c_s.at[f], c_r.at[block], target(f))

    def c_wait(b):
        return remote(pack_c.at[0], cb.at[b], c_s.at[0], c_r.at[b], source(b))

    pl.semaphore_wait(barrier, 50 - 2 * itself.astype(jnp.int32))

    for h in range(NH):
        for f in range(2):
            @pl.when(jnp.logical_not(stays(f)))
            def _():
                p1_send(h, f).start()
        if h == NH - 1:
            for f in range(2):
                @pl.when(jnp.logical_not(stays(f)))
                def _():
                    q_send(f).start()
    for f in range(2):
        @pl.when(stays(f))
        def _():
            for h in range(NH):
                kv[h, rows(me, f)] = pack_kv[f, h]
            qb[f] = pack_q[f]
            cb[f] = pack_c[f]

    over_x = {"seq": (1 - x) * NZ + z}
    up, down = {"dp": (y + 1) % 4}, {"dp": (y + 3) % 4}
    sibling = {"segment": xh * 2 + 1 - c}

    def at(dy, dx):
        return (((y + dy) % 4) * 2 + (x + dx) % 2) * 2 + c

    def ag(h, k, p, b, device):
        where = whole(p) if b is None else rows(p, b)
        return remote(
            kv.at[h, where], kv.at[h, where], ag_s.at[h, k], ag_r.at[h, p, b or 0], device
        )

    def arrived(h, p, b=None):
        ag(h, 0, p, b, over_x).wait_recv()

    sends = (
        (0, (0, 0), None, over_x), (0, (0, 0), None, up), (0, (0, 0), None, down),
        (0, (0, 0), None, sibling),
        (1, (0, 1), None, up), (1, (0, 1), None, down), (1, (0, 1), None, sibling),
        (2, (1, 0), 0, down), (2, (1, 0), None, sibling),
        (3, (3, 0), 1, up), (3, (3, 0), None, sibling),
        (4, (1, 1), None, sibling), (5, (3, 1), None, sibling),
        (6, (2, 0), None, over_x), (6, (2, 0), None, sibling),
        (7, (2, 1), None, sibling),
    )

    def stage(h, number):
        if number == 0:
            for b in range(2):
                @pl.when(jnp.logical_not(stays(b)))
                def _():
                    p1_wait(h, b).wait_recv()
        elif number == 6:
            arrived(h, at(2, 0), 0)
            arrived(h, at(2, 0), 1)
        else:
            place = next(s[1] for s in sends if s[0] == number)
            arrived(h, at(*place))
        for k, (n, place, b, device) in enumerate(sends):
            if n == number:
                ag(h, k, at(*place), b, device).start()

    zero_half = jnp.zeros((ROWS, HD), bf16)

    def both(ref, h):
        return jnp.concatenate([unfold(ref[0, h]), unfold(ref[1, h])], axis=0)

    def base_of(h, row):
        raw = both(qb, h).astype(f32)
        unit = raw * lax.rsqrt(jnp.mean(raw * raw, axis=-1, keepdims=True) + 1e-06)
        return unit * gain_ref[row:row + 1, :]

    def forward(h, query, keep):
        wide = jnp.concatenate([query * jnp.asarray(SCALE, bf16), zero_half], axis=1)
        s = lax.dot_general(wide, kv[h], (((1,), (1,)), ((), ())), preferred_element_type=f32)
        scores[...] = s
        top = s[:, :128]
        for i in range(1, KEYS // 128):
            top = jnp.maximum(top, s[:, i * 128:(i + 1) * 128])
        peak = jnp.max(top, axis=-1, keepdims=True)
        e = jnp.exp(scores[...] - peak)
        total = e[:, :128]
        for i in range(1, KEYS // 128):
            total = total + e[:, i * 128:(i + 1) * 128]
        p = e.astype(bf16)
        if keep:
            probs[...] = p
        acc = jnp.dot(p, kv[h], preferred_element_type=f32)
        total = jnp.sum(total, axis=-1, keepdims=True)
        return acc[:, HD:] / total, total

    def ac_copy(h):
        return remote(
            fo.at[h], ac.at[h], ac_s.at[h], ac_r.at[h], {"segment": (1 - xh) * 2 + c}
        )

    def rp_send(h, b):
        return remote(
            fo.at[h, b], rp.at[zq % 2, h], rp_s.at[h, b], rp_r.at[zq % 2, h], source(b)
        )

    def rp_wait(h, f):
        return remote(fo.at[h, 0], rp.at[f, h], rp_s.at[h, 0], rp_r.at[f, h], target(f))

    def give_back(h):
        for b in range(2):
            @pl.when(jnp.logical_not(stays(b)))
            def _():
                rp_send(h, b).start()

            @pl.when(stays(b))
            def _():
                rp[b, h] = fo[h, b]

    def keep_out(h, normed):
        fo[h, 0] = fold(normed[:TOK].astype(bf16))
        fo[h, 1] = fold(normed[TOK:].astype(bf16))

    def control_head(h):
        normed, _ = forward(h, base_of(h, 0).astype(bf16), False)
        keep_out(h, normed)
        ac_copy(h).start()
        give_back(h)

    def dprob_head(h):
        wide = jnp.concatenate([zero_half, both(cb, h)], axis=1)
        dprob[h] = lax.dot_general(
            wide, kv[h], (((1,), (1,)), ((), ())), preferred_element_type=f32
        )

    def main_head(h):
        base = base_of(h, 1)
        first = zq * (NH * HD) + h * HD
        tile = gate_ref[pl.ds(pl.multiple_of((first // 128) * 128, 128), 128)].reshape(1, 128)
        gate = jnp.where((zq + h) % 2 == 1, tile[:, HD:], tile[:, :HD])
        ac_copy(h).wait_recv()
        first_wide = jnp.concatenate([unfold(ac[h, 0]), unfold(ac[h, 1])], axis=0).astype(f32)
        residual = (gate * first_wide).astype(bf16)
        query = (base + residual.astype(f32)).astype(bf16)
        normed, total = forward(h, query, True)
        keep_out(h, normed)
        give_back(h)
        upstream = both(cb, h)
        delta = jnp.sum(upstream.astype(f32) * normed, axis=-1, keepdims=True)
        inverse = 1.0 / total
        ds = (probs[...].astype(f32) * inverse * (dprob[h] - delta)).astype(bf16)
        acc = jnp.dot(ds, kv[h], preferred_element_type=f32)
        rgrad = (acc[:, :HD] * SCALE).astype(bf16).astype(f32)
        part = jnp.sum(first_wide * rgrad, axis=0, keepdims=True)
        parts[pl.ds(h, 1), :] = jnp.concatenate([part, part], axis=1)

    def complete(h):
        for dy in range(4):
            for dx in range(2):
                arrived(h, at(dy, dx) + 1 - 2 * c)

    def stages(h, *numbers):
        for n in numbers:
            stage(h, n)

    stages(0, 0, 1, 2, 3)
    stages(1, 0)
    stages(0, 4, 5, 6)
    stages(1, 1, 2, 3)
    stages(2, 0)
    for f in range(2):
        @pl.when(is_main & jnp.logical_not(stays(f)))
        def _():
            c_send(f).start()
    for b in range(2):
        @pl.when(jnp.logical_not(stays(b)))
        def _():
            q_wait(b).wait_recv()
    stages(1, 4, 5, 6)
    stages(0, 7)
    complete(0)

    @pl.when(is_main)
    def _():
        stages(2, 1, 2, 3)
        stages(1, 7)
        for b in range(2):
            @pl.when(jnp.logical_not(stays(b)))
            def _():
                c_wait(b).wait_recv()
        complete(1)

        def ahead(h, carry):
            dprob_head(h)
            return carry

        lax.fori_loop(0, 2, ahead, 0)

    def heads(h, carry):
        @pl.when(jnp.logical_not(is_main))
        def _():
            @pl.when(h == 1)
            def _():
                stages(2, 1, 2, 3)
                stages(1, 7)
                complete(1)

            @pl.when(h == 2)
            def _():
                stages(2, 4, 5, 6, 7)
                complete(2)

            control_head(h)

        @pl.when(is_main)
        def _():
            @pl.when(h == 1)
            def _():
                stages(2, 4, 5, 6)

            @pl.when(h == 2)
            def _():
                stages(2, 7)
                complete(2)
                dprob_head(2)

            main_head(h)
        return carry

    lax.fori_loop(0, NH, heads, 0)

    def ar1_copy(n, p):
        return remote(
            ar1.at[p], ar1.at[p], ar1_s.at[n], ar1_r.at[p], in_row((me + n) % NP)
        )

    def ar2_copy(n, p):
        return remote(ar2.at[p], ar2.at[p], ar2_s.at[n], ar2_r.at[p], in_column(n))

    @pl.when(is_main)
    def _():
        pieces = [parts[h:h + 1, :HD] for h in range(NH)]
        ar1[me] = jnp.concatenate(pieces + [jnp.zeros((1, HD), f32)], axis=1)
        for n in range(1, NP):
            ar1_copy(n, me).start()
        for n in range(1, NP):
            ar1_copy(n, (me + n) % NP).wait_recv()
        part = ar1[0]
        for n in range(1, NP):
            part = part + ar1[n]
        ar2[z] = part
        for n in range(1, 2 * NZ):
            ar2_copy(n, z).start()
        for n in range(1, NZ):
            ar2_copy(n, (z + n) % NZ).wait_recv()

    @pl.when(jnp.logical_not(is_main))
    def _():
        for n in range(NZ):
            ar2_copy(1, n).wait_recv()

    totals = []
    for q in range(NQ):
        part = (ar2[4 * q] + ar2[4 * q + 1]) + (ar2[4 * q + 2] + ar2[4 * q + 3])
        totals.append(part[:, :NH * HD])
    whole_sum = jnp.concatenate(totals, axis=1)
    for i in range(6):
        gg_ref[i * 128:(i + 1) * 128] = whole_sum[:, i * 128:(i + 1) * 128].reshape(128)

    for f in range(2):
        @pl.when(jnp.logical_not(stays(f)))
        def _():
            for h in range(NH):
                rp_wait(h, f).wait_recv()
    for pair in range(3):
        halves = [unfold(rp[n // NH, n % NH]) for n in (2 * pair, 2 * pair + 1)]
        out_ref[0, :, pair * 128:pair * 128 + 128] = jnp.concatenate(halves, axis=1)

    for f in range(2):
        @pl.when(jnp.logical_not(stays(f)))
        def _():
            for h in range(NH):
                p1_send(h, f).wait_send()
                rp_send(h, f).wait_send()
            q_send(f).wait_send()

            @pl.when(is_main)
            def _():
                c_send(f).wait_send()
    for h in range(NH):
        for k, (n, place, b, device) in enumerate(sends):
            ag(h, k, at(*place), b, device).wait_send()

    @pl.when(jnp.logical_not(is_main))
    def _():
        for h in range(NH):
            ac_copy(h).wait_send()

    @pl.when(is_main)
    def _():
        for n in range(1, NP):
            ar1_copy(n, me).wait_send()
        for n in range(1, 2 * NZ):
            ar2_copy(n, z).wait_send()


def local(q_in, k_in, v_in, q_gain, gate, cot):
    hbm = pl.BlockSpec(memory_space=pltpu.HBM)
    vmem = pl.BlockSpec(memory_space=pltpu.VMEM)
    dma = pltpu.SemaphoreType.DMA
    out, gg = pl.pallas_call(
        kernel,
        out_shape=(
            jax.ShapeDtypeStruct(q_in.shape, bf16),
            jax.ShapeDtypeStruct(gate.shape, f32),
        ),
        in_specs=[hbm] * 3 + [vmem] * 2 + [hbm],
        out_specs=(vmem, vmem),
        scratch_shapes=[
            pltpu.VMEM(q_in.shape, bf16),
            pltpu.VMEM(k_in.shape, bf16),
            pltpu.VMEM(v_in.shape, bf16),
            pltpu.VMEM(cot.shape, bf16),
            pltpu.VMEM((2, NH, TOK, 128), bf16),
            pltpu.VMEM((2, NH, HD, 128), bf16),
            pltpu.VMEM((2, NH, HD, 128), bf16),
            pltpu.VMEM((NH, KEYS, 128), bf16),
            pltpu.VMEM((2, NH, HD, 128), bf16),
            pltpu.VMEM((2, NH, HD, 128), bf16),
            pltpu.VMEM((NH, 2, HD, 128), bf16),
            pltpu.VMEM((NH, 2, HD, 128), bf16),
            pltpu.VMEM((2, NH, HD, 128), bf16),
            pltpu.VMEM((ROWS, KEYS), f32),
            pltpu.VMEM((ROWS, KEYS), bf16),
            pltpu.VMEM((NH, ROWS, KEYS), f32),
            pltpu.VMEM((8, 128), f32),
            pltpu.VMEM((NP, 1, 256), f32),
            pltpu.VMEM((NZ, 1, 256), f32),
            dma((4,)),
            dma((2, NH)), dma((2, NH)), dma((2,)), dma((2,)), dma((2,)), dma((2,)),
            dma((NH, 16)), dma((NH, NP, 2)), dma((NH,)), dma((NH,)),
            dma((NH, 2)), dma((2, NH)),
            dma((NP,)), dma((NP,)), dma((2 * NZ,)), dma((NZ,)),
        ],
        compiler_params=pltpu.CompilerParams(
            collective_id=0, has_side_effects=True, vmem_limit_bytes=58 * 2**20
        ),
    )(q_in, k_in, v_in, q_gain, gate, cot)
    return out, gg


def solution(mesh):
    in_specs = (
        P("dp", "seq", "segment"),
        P("dp", "seq", "segment"),
        P("dp", "seq", "segment"),
        P(),
        P(),
        P("dp", "seq", None),
    )
    out_specs = (P("dp", "seq", "segment"), P())
    return jax.shard_map(local, mesh=mesh, in_specs=in_specs, out_specs=out_specs, check_vma=False)
```

time: 450 us -> 90.8 us (0.20)
  waiting for transfers between devices: 289 us -> 0 us
  blocking collectives: 124 us -> 0 us
  Pallas kernels: 0 us -> 87.8 us
  between operations: 14.2 us -> 0.65 us
  local copies, waits for them, and re-layouts: 9.4 us -> 2.14 us
  matrix products: 5.29 us -> 0 us
    all_gather x2 -> x0, waiting for transfers between devices: 249 us -> none  [the longest x1 133 us: local(): lax.all_gather(values, 'seq', axis=0, tiled=True)]
    psum x1 -> x0, blocking collectives: 124 us -> none  [local(): total_gate = lax.psum(placed, ('segment', 'seq', 'dp'))]
    pallas_call x0 -> x1, Pallas kernels: none -> 87.8 us  [local(): pl.pallas_call(kernel, out_shape=(jax.ShapeDtypeStruct(q_in.shape, bf16),...]
    ppermute x2 -> x0, waiting for transfers between devices: 39.8 us -> none  [shifted(): lax.ppermute(value, axis, [(source, source + steps) for source in range(f...]
    dot_general x6 -> x0, matrix products: 5.29 us -> none  [the longest x3 2.79 us: attend(): jnp.einsum('hqk,khd->qhd', probs, values_group, preferred_element_type=jn...]
  transfers between devices with their start and end apart: 4 -> 0, of which waited for: 4 -> 0; matrix products, arithmetic and copies ran while one was open for 1% -> 0% of each run, Pallas kernels for 0% -> 0%
where the time goes in v3:
time: 90.8 us; the launch traced here: 90.6 us
  Pallas kernels  87.8 us (97%)
  local copies, waits for them, and re-layouts  2.14 us (2%)
    pallas_call x1, Pallas kernels, local(): pl.pallas_call(kernel, out_shape=(jax.ShapeDtypeStruct(q_in.shape, bf16),...  87.8 us
    unnamed x4, local copies, waits for them, and re-layouts  2.14 us

profile of v3, /device:TPU:1, one launch (start us, length us, event | category | flops | bytes accessed | tf_op | source)
XLA Modules:
  0.0 90.6 jit_solution(11958968826314475827)
XLA Ops:
  0.6 87.8 %shard_map.77 = (bf16[1,128,384]{2,1,0:T(8,128)(2,1)}, f32[768]{0:T(1024)}) custom-call(bf16[1,128,384]{2,1,0:T(8,128)(2,1)} %q_hbm.1, bf16[1,128,384]{2,1,0:T(8,128)(2,1)} %k_hbm.1, bf16[1,128,384]{2,1,0:T(8,128)(2,1)} %v_hbm.1, f32[2,64]{1,0:T(2,128)} %gain_ref.1, f32[768]{0:T(1024)} %gate_ref.1, bf16[1,128,768]{2,1,0:T(8,128)(2,1)} %cot_hbm.1), custom_call_target="tpu_custom_call" | custom-call | tf_op jit(solution)/shard_map/pallas_call | solution.py:446
  88.5 0.0 copy-start
  88.5 1.5 %copy.10 = bf16[1,128,384]{2,1,0:T(8,128)(2,1)} copy(bf16[1,128,384]{2,1,0:T(8,128)(2,1)} %get-tuple-element.4) | data formatting | bytes 196608
  90.0 0.0 copy-done
  90.0 0.6 copy.11
Async XLA Ops:
  88.5 1.6 %copy-start = (f32[768]{0:T(1024)S(1)}, f32[768]{0:T(1024)}, u32[]{:S(2)}) copy-start(f32[768]{0:T(1024)} %get-tuple-element.5) | copy-start | bytes 9220

commit v4 on v3

--- a/solution.py
+++ b/solution.py
@@ -37,7 +37,7 @@
     x, z = seq // NZ, seq % NZ
     is_main = xh == 1
     zq, zs = z // 4, z % 4
-    me = (y * 2 + x) * 2 + c
+    me = (c * 4 + y) * 2 + x
     itself = z == 12 * c + y
 
     loads = [
@@ -56,7 +56,7 @@
         return {"segment": xh * 2 + zq // 2, "seq": x * NZ + y + 4 * c + 8 * b, "dp": zs}
 
     def in_row(p):
-        return {"segment": xh * 2 + p % 2, "seq": ((p // 2) % 2) * NZ + z, "dp": p // 4}
+        return {"segment": xh * 2 + p // 8, "seq": (p % 2) * NZ + z, "dp": (p // 2) % 4}
 
     def in_column(n):
         there = (xh * NZ + z + n) % (2 * NZ)
@@ -111,7 +111,7 @@
             device_id=device, device_id_type=MESH,
         )
 
-    there = (zs * 2 + x) * 2 + zq % 2
+    there = ((zq % 2) * 4 + zs) * 2 + x
     block = zq // 2
 
     def p1_send(h, f):
@@ -140,12 +140,16 @@
     pl.semaphore_wait(barrier, 50 - 2 * itself.astype(jnp.int32))
 
     for h in range(NH):
-        for f in range(2):
+        for n in range(2):
+            f = (n + z) % 2
+
             @pl.when(jnp.logical_not(stays(f)))
             def _():
                 p1_send(h, f).start()
         if h == NH - 1:
-            for f in range(2):
+            for n in range(2):
+                f = (n + z) % 2
+
                 @pl.when(jnp.logical_not(stays(f)))
                 def _():
                     q_send(f).start()
@@ -162,7 +166,7 @@
     sibling = {"segment": xh * 2 + 1 - c}
 
     def at(dy, dx):
-        return (((y + dy) % 4) * 2 + (x + dx) % 2) * 2 + c
+        return (c * 4 + (y + dy) % 4) * 2 + (x + dx) % 2
 
     def ag(h, k, p, b, device):
         where = whole(p) if b is None else rows(p, b)
@@ -170,19 +174,24 @@
             kv.at[h, where], kv.at[h, where], ag_s.at[h, k], ag_r.at[h, p, b or 0], device
         )
 
+    def beside(h, k, core, dy):
+        p = (core * 4 + (y + dy) % 4) * 2
+        where = pl.ds(pl.multiple_of(p * ROWS, 2 * ROWS), 2 * ROWS)
+        return remote(
+            kv.at[h, where], kv.at[h, where], ag_s.at[h, k], ag_r.at[h, p, 0], sibling
+        )
+
     def arrived(h, p, b=None):
         ag(h, 0, p, b, over_x).wait_recv()
 
     sends = (
         (0, (0, 0), None, over_x), (0, (0, 0), None, up), (0, (0, 0), None, down),
-        (0, (0, 0), None, sibling),
-        (1, (0, 1), None, up), (1, (0, 1), None, down), (1, (0, 1), None, sibling),
-        (2, (1, 0), 0, down), (2, (1, 0), None, sibling),
-        (3, (3, 0), 1, up), (3, (3, 0), None, sibling),
-        (4, (1, 1), None, sibling), (5, (3, 1), None, sibling),
-        (6, (2, 0), None, over_x), (6, (2, 0), None, sibling),
-        (7, (2, 1), None, sibling),
+        (1, (0, 1), None, up), (1, (0, 1), None, down),
+        (2, (1, 0), 0, down), (3, (3, 0), 1, up),
+        (6, (2, 0), None, over_x),
     )
+    places = {1: (0, 1), 2: (1, 0), 3: (3, 0), 4: (1, 1), 5: (3, 1), 7: (2, 1)}
+    siblings = {1: (8, 0), 4: (9, 1), 5: (10, 3), 7: (11, 2)}
 
     def stage(h, number):
         if number == 0:
@@ -194,11 +203,13 @@
             arrived(h, at(2, 0), 0)
             arrived(h, at(2, 0), 1)
         else:
-            place = next(s[1] for s in sends if s[0] == number)
-            arrived(h, at(*place))
+            arrived(h, at(*places[number]))
         for k, (n, place, b, device) in enumerate(sends):
             if n == number:
                 ag(h, k, at(*place), b, device).start()
+        if number in siblings:
+            k, dy = siblings[number]
+            beside(h, k, c, dy).start()
 
     zero_half = jnp.zeros((ROWS, HD), bf16)
 
@@ -291,8 +302,7 @@
 
     def complete(h):
         for dy in range(4):
-            for dx in range(2):
-                arrived(h, at(dy, dx) + 1 - 2 * c)
+            beside(h, 0, 1 - c, dy).wait_recv()
 
     def stages(h, *numbers):
         for n in numbers:
@@ -425,6 +435,8 @@
     for h in range(NH):
         for k, (n, place, b, device) in enumerate(sends):
             ag(h, k, at(*place), b, device).wait_send()
+        for k, dy in siblings.values():
+            beside(h, k, c, dy).wait_send()
 
     @pl.when(jnp.logical_not(is_main))
     def _():

time: 90.8 us -> 90.4 us (level)
  no operation moved by 1% of the time
where the time goes in v4:
time: 90.4 us; the launch traced here: 90.2 us
  Pallas kernels  87.4 us (97%)
  local copies, waits for them, and re-layouts  2.14 us (2%)
    pallas_call x1, Pallas kernels, local(): pl.pallas_call(kernel, out_shape=(jax.ShapeDtypeStruct(q_in.shape, bf16),...  87.4 us
    unnamed x4, local copies, waits for them, and re-layouts  2.14 us

profile of v4, /device:TPU:1, one launch (start us, length us, event | category | flops | bytes accessed | tf_op | source)
XLA Modules:
  0.0 90.2 jit_solution(16492718602001503920)
XLA Ops:
  0.6 87.4 %shard_map.77 = (bf16[1,128,384]{2,1,0:T(8,128)(2,1)}, f32[768]{0:T(1024)}) custom-call(bf16[1,128,384]{2,1,0:T(8,128)(2,1)} %q_hbm.1, bf16[1,128,384]{2,1,0:T(8,128)(2,1)} %k_hbm.1, bf16[1,128,384]{2,1,0:T(8,128)(2,1)} %v_hbm.1, f32[2,64]{1,0:T(2,128)} %gain_ref.1, f32[768]{0:T(1024)} %gate_ref.1, bf16[1,128,768]{2,1,0:T(8,128)(2,1)} %cot_hbm.1), custom_call_target="tpu_custom_call" | custom-call | tf_op jit(solution)/shard_map/pallas_call | solution.py:458
  88.1 0.0 copy-start
  88.1 1.5 %copy.10 = bf16[1,128,384]{2,1,0:T(8,128)(2,1)} copy(bf16[1,128,384]{2,1,0:T(8,128)(2,1)} %get-tuple-element.4) | data formatting | bytes 196608
  89.6 0.0 copy-done
  89.6 0.6 copy.11
Async XLA Ops:
  88.1 1.6 %copy-start = (f32[768]{0:T(1024)S(1)}, f32[768]{0:T(1024)}, u32[]{:S(2)}) copy-start(f32[768]{0:T(1024)} %get-tuple-element.5) | copy-start | bytes 9220

commit v5 on v4

--- a/solution.py
+++ b/solution.py
@@ -25,7 +25,7 @@
 def kernel(
     q_hbm, k_hbm, v_hbm, gain_ref, gate_ref, cot_hbm,
     out_ref, gg_ref,
-    q_ref, k_ref, v_ref, cot_ref,
+    q_ref, k_ref, v_ref, cot_ref, out_v, out_s,
     pack_kv, pack_q, pack_c, kv, qb, cb, ac, fo, rp, scores, probs, dprob, parts, ar1, ar2,
     load_s, p1_s, p1_r, q_s, q_r, c_s, c_r, ag_s, ag_r, ac_s, ac_r, rp_s, rp_r,
     ar1_s, ar1_r, ar2_s, ar2_r,
@@ -396,6 +396,21 @@
         ar2[z] = part
         for n in range(1, 2 * NZ):
             ar2_copy(n, z).start()
+
+    for f in range(2):
+        @pl.when(jnp.logical_not(stays(f)))
+        def _():
+            for h in range(NH):
+                rp_wait(h, f).wait_recv()
+    for pair in range(3):
+        halves = [unfold(rp[n // NH, n % NH]) for n in (2 * pair, 2 * pair + 1)]
+        out_v[0, :, pair * 128:pair * 128 + 128] = jnp.concatenate(halves, axis=1)
+
+    out_copy = pltpu.make_async_copy(out_v, out_ref, out_s)
+    out_copy.start()
+
+    @pl.when(is_main)
+    def _():
         for n in range(1, NZ):
             ar2_copy(n, (z + n) % NZ).wait_recv()
 
@@ -412,15 +427,7 @@
     for i in range(6):
         gg_ref[i * 128:(i + 1) * 128] = whole_sum[:, i * 128:(i + 1) * 128].reshape(128)
 
-    for f in range(2):
-        @pl.when(jnp.logical_not(stays(f)))
-        def _():
-            for h in range(NH):
-                rp_wait(h, f).wait_recv()
-    for pair in range(3):
-        halves = [unfold(rp[n // NH, n % NH]) for n in (2 * pair, 2 * pair + 1)]
-        out_ref[0, :, pair * 128:pair * 128 + 128] = jnp.concatenate(halves, axis=1)
-
+    out_copy.wait()
     for f in range(2):
         @pl.when(jnp.logical_not(stays(f)))
         def _():
@@ -462,12 +469,14 @@
             jax.ShapeDtypeStruct(gate.shape, f32),
         ),
         in_specs=[hbm] * 3 + [vmem] * 2 + [hbm],
-        out_specs=(vmem, vmem),
+        out_specs=(hbm, vmem),
         scratch_shapes=[
             pltpu.VMEM(q_in.shape, bf16),
             pltpu.VMEM(k_in.shape, bf16),
             pltpu.VMEM(v_in.shape, bf16),
             pltpu.VMEM(cot.shape, bf16),
+            pltpu.VMEM(q_in.shape, bf16),
+            pltpu.SemaphoreType.DMA,
             pltpu.VMEM((2, NH, TOK, 128), bf16),
             pltpu.VMEM((2, NH, HD, 128), bf16),
             pltpu.VMEM((2, NH, HD, 128), bf16),

time: 90.4 us -> 90.2 us (level)
  no operation moved by 1% of the time
where the time goes in v5:
time: 90.2 us; the launch traced here: 90 us
  Pallas kernels  87.2 us (97%)
  local copies, waits for them, and re-layouts  2.14 us (2%)
    pallas_call x1, Pallas kernels, local(): pl.pallas_call(kernel, out_shape=(jax.ShapeDtypeStruct(q_in.shape, bf16),...  87.2 us
    unnamed x4, local copies, waits for them, and re-layouts  2.14 us

profile of v5, /device:TPU:1, one launch (start us, length us, event | category | flops | bytes accessed | tf_op | source)
XLA Modules:
  0.0 90.0 jit_solution(17707222631737404251)
XLA Ops:
  0.6 87.2 %shard_map.77 = (bf16[1,128,384]{2,1,0:T(8,128)(2,1)}, f32[768]{0:T(1024)}) custom-call(bf16[1,128,384]{2,1,0:T(8,128)(2,1)} %q_hbm.1, bf16[1,128,384]{2,1,0:T(8,128)(2,1)} %k_hbm.1, bf16[1,128,384]{2,1,0:T(8,128)(2,1)} %v_hbm.1, f32[2,64]{1,0:T(2,128)} %gain_ref.1, f32[768]{0:T(1024)} %gate_ref.1, bf16[1,128,768]{2,1,0:T(8,128)(2,1)} %cot_hbm.1), custom_call_target="tpu_custom_call" | custom-call | tf_op jit(solution)/shard_map/pallas_call | solution.py:465
  87.9 0.0 copy-start
  87.9 1.5 %copy.10 = bf16[1,128,384]{2,1,0:T(8,128)(2,1)} copy(bf16[1,128,384]{2,1,0:T(8,128)(2,1)} %get-tuple-element.4) | data formatting | bytes 196608
  89.4 0.0 copy-done
  89.4 0.6 copy.11
Async XLA Ops:
  87.9 1.6 %copy-start = (f32[768]{0:T(1024)S(1)}, f32[768]{0:T(1024)}, u32[]{:S(2)}) copy-start(f32[768]{0:T(1024)} %get-tuple-element.5) | copy-start | bytes 9220
